TPU v7x, 128 devices: a whole 4x4x4 slice. The times are simulated.
128 devices in a mesh: aux: 64 (over z, y, x), bas: 2 (over core).
Axes of the slice: x: 4, y: 4, z: 4, core: 2. Of those that a mesh axis runs over, the one named last changes fastest.
Arguments:
- integrals: bfloat16 [64, 128, 3, 128, 128], P('aux', 'bas'), may hold values from -0.0625 to 0.0625
- orbitals: bfloat16 [128, 128, 128], P('bas'), may hold values from -0.5 to 0.5
- locality: int32 [128], P('bas'), may hold values from 0 to 63, as said below
- screen: int32 [64, 128, 3], P('aux', 'bas'), may hold values 0 or 1
- metric: bfloat16 [64, 64], replicated, may hold values from -1 to 3
Outputs:
- exchange_band: float32 [128, 5, 16384], P('bas', None, 'aux')
Inputs may be any that keep to these rules, and one draw needn't show every extreme that they name: `locality`: within each bas shard, its 64 orbital tiles name each of its 64 blocks exactly once.
All inputs are finite; a program needn't handle non-finite values. No bound on the sum of `screen` on one device may be relied on, other than what follows from the above.
Results may differ from a plain program's by a relative error of at most 0.00096.
Values may be sent and summed in bfloat16 or wider, within the bound.
A program may use at most 128 MiB of HBM per device.

v0:
```python
import jax
import jax.numpy as jnp
from jax import lax
from jax.sharding import PartitionSpec as P


def passed_along(value, axis, steps):
    count = lax.axis_size(axis)
    first, last = (max(0, -steps), min(count, count - steps))
    return lax.ppermute(value, axis, [(source, source + steps) for source in range(first, last)])


def metric_apply(metric, exchanged):
    slab_rows = exchanged[0]
    product = jnp.dot(
        metric, slab_rows.reshape(slab_rows.shape[0], -1), preferred_element_type=jnp.float32
    )
    results = [product.astype(jnp.bfloat16).reshape(slab_rows.shape)]
    return jnp.stack(results)


def add_band(window, gram_block, row_first):
    reach_width = gram_block.shape[0]
    for offset in range(reach_width):
        band_piece = jnp.transpose(gram_block[offset], (1, 0, 2))
        band_piece = jnp.pad(band_piece, ((reach_width - 1 - offset, offset), (0, 0), (0, 0)))
        start_row = row_first + offset
        current = lax.dynamic_slice_in_dim(window, start_row, 1, 0)
        window = lax.dynamic_update_slice_in_dim(window, current + band_piece[None], start_row, 0)
    return window


def body(integrals, orbitals, locality, screen, metric):
    aux_rows, block_count, reach_width, tile_size, _ = integrals.shape
    reach_blocks = reach_width // 2
    orbital_count = orbitals.shape[0]
    per_device = orbital_count // lax.axis_size("aux")
    first_block = lax.axis_index("bas") * block_count
    total_blocks = block_count * lax.axis_size("bas")
    chosen = jnp.take(integrals, locality, axis=1)
    half_rows = lax.dot_general(
        chosen, orbitals, (((4,), (1,)), ((1,), (0,))), preferred_element_type=jnp.float32
    )
    offsets = jnp.arange(reach_width, dtype=jnp.int32)
    row_blocks = first_block + locality[:, None] + offsets[None, :] - reach_blocks
    inside = ((row_blocks >= 0) & (row_blocks < total_blocks)).astype(jnp.float32)
    keep_mask = screen[0].astype(jnp.float32) * inside
    half_rows = (half_rows * keep_mask[:, None, :, None, None]).astype(jnp.bfloat16)
    mixed_rows = metric_apply(
        metric, lax.all_to_all(half_rows, "aux", split_axis=0, concat_axis=1, tiled=True)
    )
    mine = lax.dynamic_slice_in_dim(locality, lax.axis_index("aux") * per_device, per_device, 0)
    window = jnp.zeros(
        (block_count + 2 * reach_blocks, 2 * reach_width - 1, tile_size, tile_size), jnp.float32
    )
    fitted = mixed_rows[0]
    gram_block = lax.dot_general(
        fitted, fitted, (((0, 3), (0, 3)), ((), ())), preferred_element_type=jnp.float32
    )
    window = add_band(window, gram_block, mine[0])
    lower_rim = window[:reach_blocks]
    upper_rim = window[reach_blocks + block_count :]
    own_rows = window[reach_blocks : reach_blocks + block_count]
    from_below = passed_along(upper_rim.astype(jnp.bfloat16), "bas", 1).astype(upper_rim.dtype)
    from_above = passed_along(lower_rim.astype(jnp.bfloat16), "bas", -1).astype(lower_rim.dtype)
    own_rows = own_rows.at[:reach_blocks].add(from_below)
    own_rows = own_rows.at[block_count - reach_blocks :].add(from_above)
    flat_rows = own_rows.reshape(block_count, 2 * reach_width - 1, tile_size * tile_size)
    return lax.psum_scatter(flat_rows, "aux", scatter_dimension=2, tiled=True)


def solution(mesh):
    placed = (
        P("aux", "bas", None, None, None),
        P("bas", None, None),
        P("bas"),
        P("aux", "bas", None),
        P(),
    )
    return jax.shard_map(
        body, mesh=mesh, in_specs=placed, out_specs=P("bas", None, "aux"), check_vma=False
    )
```

profile of v0, /device:TPU:0, one launch (start us, length us, event | category | flops | bytes accessed | tf_op | source)
XLA Modules:
  0.0 615.3 jit_solution(4274369219538918507)
XLA Ops:
  6.5 0.0 copy-start
  6.5 0.8 compare_and_fusion
  7.3 0.7 compare_select_fusion
  8.0 0.7 convert_element_type.37
  8.7 0.1 copy.14
  8.8 6.8 %gather_fusion = bf16[64,3,128,128]{3,2,1,0:T(8,128)(2,1)} fusion(bf16[64,3,128,128]{3,2,1,0:T(8,128)(2,1)} %bitcast.62, s32[1024]{0:T(1024)S(1)} %pad_clamp_fusion), kind=kCustom, calls=%fused_computation | custom fusion | bytes 12583168 | tf_op jit(solution)/shard_map/jit(_take)/gather | solution.py:40
  15.6 0.0 copy-done
  15.6 7.3 %fusion = bf16[64,1,3,128,128]{4,3,2,1,0:T(8,128)(2,1)} fusion(f32[64,3]{1,0:T(8,128)S(1)} %copy.14, bf16[64,3,128,128]{3,2,1,0:T(8,128)(2,1)} %gather_fusion, pred[64]{0:T(512)(128)(4,1)S(1)} %compare_and_fusion, bf16[64,128,128]{2,1,0:T(8,128)(2,1)S(1)} %copy-done), kind=kOutput, calls=%fused_computation.3 | convolution fusion | flops 814743552 | bytes 14680896 | tf_op jit(solution)/shard_map/dot_general | solution.py:41
  22.9 0.0 copy-start.4
  22.9 0.0 copy-start.3
  22.9 11.9 %all-to-all-start = ((bf16[64,1,3,128,128]{4,3,2,1,0:T(8,128)(2,1)}), bf16[64,1,3,128,128]{4,3,2,1,0:T(8,128)(2,1)}, u32[]{:S(2)}, u32[]{:S(2)}) async-start(bf16[64,1,3,128,128]{4,3,2,1,0:T(8,128)(2,1)} %fusion), calls=%async_computation | async-start | bytes 12582912 | tf_op jit(solution)/shard_map/all_to_all | solution.py:50
  34.7 0.2 reduce-scatter.2.cloned.1.call-start
  35.0 0.0 copy-done.4
  35.0 0.6 dynamic_slice.9
  40.1 75.4 %all-to-all-done = bf16[64,1,3,128,128]{4,3,2,1,0:T(8,128)(2,1)} async-done(((bf16[64,1,3,128,128]{4,3,2,1,0:T(8,128)(2,1)}), bf16[64,1,3,128,128]{4,3,2,1,0:T(8,128)(2,1)}, u32[]{:S(2)}, u32[]{:S(2)}) %all-to-all-start) | async-done | bytes 6291488 | tf_op jit(solution)/shard_map/all_to_all | solution.py:50
  115.5 0.0 copy-done.3
  115.5 7.7 %fusion.13 = bf16[8,8,384,128]{3,1,2,0:T(8,128)(2,1)S(1)} fusion(bf16[64,64]{1,0:T(8,128)(2,1)S(1)} %copy-done.3, bf16[8,8,384,128]{3,2,1,0:T(8,128)(2,1)} %bitcast.27), kind=kOutput, calls=%fused_computation.14 | convolution fusion | flops 405798912 | bytes 12591104 | tf_op jit(solution)/shard_map/dot_general | solution.py:15
  123.1 1.7 copy.26
  124.9 3.4 fusion.17
  128.4 9.9 %broadcast_in_dim.27 = f32[66,5,128,128]{3,2,1,0:T(8,128)} broadcast(f32[]{:T(128)} %constant.85.clone.1), dimensions={} | broadcast | bytes 21626884 | tf_op jit(solution)/shard_map/broadcast_in_dim | solution.py:53
  138.3 0.8 bitcast_dynamic-update-slice_fusion
  139.0 1.8 fusion.25
  140.8 1.7 fusion.24
  142.5 0.0 copy-start.2
  142.5 8.6 %convert.4 = bf16[66,5,128,128]{3,2,1,0:T(8,128)(2,1)S(1)} convert(f32[66,5,128,128]{3,2,1,0:T(8,128)} %fusion.24) | non-fusion elementwise | flops 5406720 | bytes 32440320 | tf_op jit(solution)/shard_map/convert.1
  151.1 1.6 collective-permute-start
  152.7 3.2 copy-done.2
  155.9 7.4 %slice.92 = f32[64,5,128,128]{3,2,1,0:T(8,128)} slice(f32[66,5,128,128]{3,2,1,0:T(8,128)S(1)} %copy-done.2), slice={[1:65], [0:5], [0:128], [0:128]} | slice | bytes 41943040 | tf_op jit(solution)/shard_map/slice | solution.py:63
  163.3 1.3 collective-permute-start.1
  164.6 0.0 collective-permute-done
  164.6 0.8 fusion.23
  165.4 1.2 collective-permute-done.1
  166.6 1.7 fusion.22
  168.3 16.1 %copy.18 = f32[64,5,128,128]{3,2,0,1:T(8,128)} copy(f32[64,5,128,128]{3,2,1,0:T(8,128)} %fusion.22) | data formatting | bytes 41943040 | tf_op jit(solution)/shard_map/scatter-add | solution.py:67
  184.4 22.7 %reshape.123 = f32[64,5,16384]{2,0,1:T(8,128)} reshape(f32[64,5,128,128]{3,2,0,1:T(8,128)} %copy.18) | data formatting | bytes 41943040 | tf_op jit(solution)/shard_map/reshape | solution.py:68
  207.1 0.0 copy-start.1
  207.1 0.0 reduce-scatter.2.cloned.1.call-update
  207.1 401.3 %reduce-scatter.2.cloned.1.call-done = f32[64,5,256]{2,0,1:T(8,128)} async-done(((f32[64,5,16384]{2,0,1:T(8,128)}), f32[64,5,256]{2,0,1:T(8,128)}) %reduce-scatter.2.cloned.1.call-update) | async-done | bytes 327696 | tf_op jit(solution)/shard_map/reduce_scatter | solution.py:69
  608.4 0.0 copy-done.1
  (4 shorter events, 0.1 us)
Async XLA Ops:
  6.5 9.0 %copy-start = (bf16[64,128,128]{2,1,0:T(8,128)(2,1)S(1)}, bf16[64,128,128]{2,1,0:T(8,128)(2,1)}, u32[]{:S(2)}) copy-start(bf16[64,128,128]{2,1,0:T(8,128)(2,1)} %param.10) | copy-start | bytes 6291460
  22.9 12.1 %copy-start.4 = (s32[64]{0:T(128)S(1)}, s32[64]{0:T(128)}, u32[]{:S(2)}) copy-start(s32[64]{0:T(128)} %param.11) | copy-start | bytes 772
  22.9 92.6 %copy-start.3 = (bf16[64,64]{1,0:T(8,128)(2,1)S(1)}, bf16[64,64]{1,0:T(8,128)(2,1)}, u32[]{:S(2)}) copy-start(bf16[64,64]{1,0:T(8,128)(2,1)} %param.13) | copy-start | bytes 24580
  22.9 92.6 %all-to-all-start = ((bf16[64,1,3,128,128]{4,3,2,1,0:T(8,128)(2,1)}), bf16[64,1,3,128,128]{4,3,2,1,0:T(8,128)(2,1)}, u32[]{:S(2)}, u32[]{:S(2)}) async-start(bf16[64,1,3,128,128]{4,3,2,1,0:T(8,128)(2,1)} %fusion), calls=%async_computation | async-start | bytes 12582912 | tf_op jit(solution)/shard_map/all_to_all | solution.py:50
  34.7 573.7 %reduce-scatter.2.cloned.1.call-start = ((), (), s32[]{:S(2)}) async-start(), calls=%async_computation.2 | async-start | bytes 21299200 | tf_op jit(solution)/shard_map/reduce_scatter | solution.py:69
  142.5 13.4 %copy-start.2 = (f32[66,5,128,128]{3,2,1,0:T(8,128)S(1)}, f32[66,5,128,128]{3,2,1,0:T(8,128)}, u32[]{:S(2)}) copy-start(f32[66,5,128,128]{3,2,1,0:T(8,128)} %fusion.24) | copy-start | bytes 64880644
  151.1 13.5 %collective-permute-start = (bf16[1,5,128,128]{3,2,1,0:T(8,128)(2,1)S(1)}, bf16[1,5,128,128]{3,2,1,0:T(8,128)(2,1)S(1)}, u32[]{:S(2)}, u32[]{:S(2)}) collective-permute-start(bf16[1,5,128,128]{3,2,1,0:T(8,128)(2,1)S(1)} %get-tuple-element.30), channel_id=1, source_target_pairs={{0,1},{2,3},{4,5},{6,7},{8,9},{10,11},{12,13},{14,15},{16,17},{18,... | collective-permute-start | bytes 491528 | tf_op jit(solution)/shard_map/ppermute | solution.py:10
  163.3 3.3 collective-permute-start.1
  207.1 401.3 %copy-start.1 = (bf16[64,128,128]{2,1,0:T(8,128)(2,1)S(1)}, bf16[64,128,128]{2,1,0:T(8,128)(2,1)}, u32[]{:S(2)}) copy-start(bf16[64,128,128]{2,1,0:T(8,128)(2,1)} %param.10) | copy-start | bytes 6291460
Sparse Core Ops, SparseCore 0:
  207.2 401.1 reduce-scatter.1
where the time goes:
time: 616 us; the launch traced here: 615 us
  waiting for transfers between devices  478 us (78%)
  local copies, waits for them, and re-layouts  69.3 us (11%)
  matrix products  18.4 us (3%)
  between operations  18 us (3%)
  other arithmetic  16.7 us (3%)
  starting transfers between devices  14.9 us (2%)
    reduce_scatter x1, waiting for transfers between devices, body(): return lax.psum_scatter(flat_rows, 'aux', scatter_dimension=2, tiled=True)  401 us
    all_to_all x1, waiting for transfers between devices, body(): lax.all_to_all(half_rows, 'aux', split_axis=0, concat_axis=1, tiled=True)  75.4 us
    reshape x1, local copies, waits for them, and re-layouts, body(): own_rows.reshape(block_count, 2 * reach_width - 1, tile_size * tile_size)  22.7 us
    scatter-add x1, local copies, waits for them, and re-layouts, body(): own_rows = own_rows.at[block_count - reach_blocks:].add(from_above)  16.1 us
  transfers between devices with their start and end apart: 4, of which 3 were waited for; matrix products, arithmetic and copies ran while one was open for 1% of the time, Pallas kernels for 0%

commit v1 on v0

--- a/solution.py
+++ b/solution.py
@@ -2,6 +2,13 @@
 import jax.numpy as jnp
 from jax import lax
 from jax.sharding import PartitionSpec as P
+
+
+def swap_blocks(block, mesh_axis, split, join):
+    devices = lax.axis_size(mesh_axis)
+    tiles = jnp.stack(jnp.split(block, devices, axis=split), axis=0)
+    tiles = lax.all_to_all(tiles, mesh_axis, split_axis=0, concat_axis=0)
+    return jnp.concatenate(tiles, axis=join)
 
 
 def passed_along(value, axis, steps):
@@ -46,9 +53,7 @@
     inside = ((row_blocks >= 0) & (row_blocks < total_blocks)).astype(jnp.float32)
     keep_mask = screen[0].astype(jnp.float32) * inside
     half_rows = (half_rows * keep_mask[:, None, :, None, None]).astype(jnp.bfloat16)
-    mixed_rows = metric_apply(
-        metric, lax.all_to_all(half_rows, "aux", split_axis=0, concat_axis=1, tiled=True)
-    )
+    mixed_rows = metric_apply(metric, swap_blocks(half_rows, "aux", 0, 1))
     mine = lax.dynamic_slice_in_dim(locality, lax.axis_index("aux") * per_device, per_device, 0)
     window = jnp.zeros(
         (block_count + 2 * reach_blocks, 2 * reach_width - 1, tile_size, tile_size), jnp.float32

time: 616 us -> 655 us (1.063)
  local copies, waits for them, and re-layouts: 69.3 us -> 111 us
    unnamed x11 -> x74, local copies, waits for them, and re-layouts: 4.98 us -> 45.8 us
where the time goes in v1:
time: 655 us; the launch traced here: 654 us
  waiting for transfers between devices  478 us (73%)
  local copies, waits for them, and re-layouts  111 us (17%)
  between operations  18.1 us (3%)
  other arithmetic  16.7 us (3%)
  matrix products  15.7 us (2%)
  starting transfers between devices  14.9 us (2%)
    reduce_scatter x1, waiting for transfers between devices, body(): return lax.psum_scatter(flat_rows, 'aux', scatter_dimension=2, tiled=True)  401 us
    all_to_all x1, waiting for transfers between devices, swap_blocks(): tiles = lax.all_to_all(tiles, mesh_axis, split_axis=0, concat_axis=0)  75.4 us
    unnamed x74, local copies, waits for them, and re-layouts  45.8 us
    reshape x1, local copies, waits for them, and re-layouts, body(): own_rows.reshape(block_count, 2 * reach_width - 1, tile_size * tile_size)  22.7 us
    scatter-add x1, local copies, waits for them, and re-layouts, body(): own_rows = own_rows.at[block_count - reach_blocks:].add(from_above)  16.1 us
  transfers between devices with their start and end apart: 4, of which 3 were waited for; matrix products, arithmetic and copies ran while one was open for 1% of the time, Pallas kernels for 0%

profile of v1, /device:TPU:0, one launch (start us, length us, event | category | flops | bytes accessed | tf_op | source)
XLA Modules:
  0.0 653.9 jit_solution(17973516726043903255)
XLA Ops:
  6.5 0.8 compare_and_fusion
  7.3 0.7 compare_select_fusion
  8.0 0.7 convert_element_type.35
  8.8 6.8 %gather_fusion = bf16[64,3,128,128]{3,2,1,0:T(8,128)(2,1)} fusion(bf16[64,3,128,128]{3,2,1,0:T(8,128)(2,1)} %bitcast.314, s32[1024]{0:T(1024)S(1)} %pad_clamp_fusion), kind=kCustom, calls=%fused_computation | custom fusion | bytes 12583168 | tf_op jit(solution)/shard_map/jit(_take)/gather | solution.py:47
  15.6 4.6 multiply_convert_fusion
  20.2 0.6 constant_dynamic-update-slice_fusion.63
  20.9 0.6 constant_dynamic-update-slice_fusion.62
  21.5 0.6 constant_dynamic-update-slice_fusion.61
  22.2 0.6 constant_dynamic-update-slice_fusion.60
  22.8 0.7 constant_dynamic-update-slice_fusion.59
  24.8 0.7 constant_dynamic-update-slice_fusion.56
  25.4 0.6 constant_dynamic-update-slice_fusion.55
  26.1 0.6 constant_dynamic-update-slice_fusion.54
  27.4 0.7 constant_dynamic-update-slice_fusion.52
  29.9 0.7 constant_dynamic-update-slice_fusion.48
  30.6 0.7 constant_dynamic-update-slice_fusion.47
  31.2 0.6 constant_dynamic-update-slice_fusion.46
  31.9 0.7 constant_dynamic-update-slice_fusion.45
  32.6 0.7 constant_dynamic-update-slice_fusion.44
  33.2 0.6 constant_dynamic-update-slice_fusion.43
  33.9 0.7 constant_dynamic-update-slice_fusion.42
  35.2 0.7 constant_dynamic-update-slice_fusion.40
  35.8 0.7 constant_dynamic-update-slice_fusion.39
  36.5 0.7 constant_dynamic-update-slice_fusion.38
  37.1 0.7 constant_dynamic-update-slice_fusion.37
  37.8 0.7 constant_dynamic-update-slice_fusion.36
  39.7 0.7 constant_dynamic-update-slice_fusion.33
  41.0 0.6 constant_dynamic-update-slice_fusion.31
  42.3 0.7 constant_dynamic-update-slice_fusion.29
  44.9 0.6 constant_dynamic-update-slice_fusion.25
  46.8 0.7 constant_dynamic-update-slice_fusion.22
  47.5 0.6 constant_dynamic-update-slice_fusion.21
  48.1 0.6 constant_dynamic-update-slice_fusion.20
  49.4 0.7 constant_dynamic-update-slice_fusion.18
  50.7 0.7 constant_dynamic-update-slice_fusion.16
  53.3 0.6 constant_dynamic-update-slice_fusion.12
  54.6 0.6 constant_dynamic-update-slice_fusion.10
  55.2 0.6 constant_dynamic-update-slice_fusion.9
  55.8 0.6 constant_dynamic-update-slice_fusion.8
  56.5 0.6 constant_dynamic-update-slice_fusion.7
  58.4 0.7 constant_dynamic-update-slice_fusion.4
  59.1 0.7 constant_dynamic-update-slice_fusion.3
  59.7 0.7 constant_dynamic-update-slice_fusion.2
  60.4 0.7 constant_dynamic-update-slice_fusion.1
  61.7 11.9 %all-to-all-start = ((bf16[64,1,1,3,128,128]{5,4,3,2,1,0:T(8,128)(2,1)}), bf16[64,1,1,3,128,128]{5,4,3,2,1,0:T(8,128)(2,1)}, u32[]{:S(2)}, u32[]{:S(2)}) async-start(bf16[64,1,1,3,128,128]{5,4,3,2,1,0:T(8,128)(2,1)} %constant_dynamic-update-slice_fusion), calls=%async_computation | async-start | bytes 12582912 | tf_op jit(solution)/shard_map/all_to_all | solution.py:10
  78.9 75.4 %all-to-all-done = bf16[64,1,1,3,128,128]{5,4,3,2,1,0:T(8,128)(2,1)} async-done(((bf16[64,1,1,3,128,128]{5,4,3,2,1,0:T(8,128)(2,1)}), bf16[64,1,1,3,128,128]{5,4,3,2,1,0:T(8,128)(2,1)}, u32[]{:S(2)}, u32[]{:S(2)}) %all-to-all-start) | async-done | bytes 6291488 | tf_op jit(solution)/shard_map/all_to_all | solution.py:10
  154.3 7.7 %fusion.12 = bf16[8,8,384,128]{3,1,2,0:T(8,128)(2,1)S(1)} fusion(bf16[64,64]{1,0:T(8,128)(2,1)S(1)} %copy-done.3, bf16[8,8,384,128]{3,2,1,0:T(8,128)(2,1)} %bitcast.88), kind=kOutput, calls=%fused_computation.13 | convolution fusion | flops 405798912 | bytes 12591104 | tf_op jit(solution)/shard_map/dot_general | solution.py:22
  162.0 1.7 copy.21
  163.7 3.4 fusion.16
  167.2 9.9 %broadcast_in_dim.27 = f32[66,5,128,128]{3,2,1,0:T(8,128)} broadcast(f32[]{:T(128)} %constant.85.clone.1), dimensions={} | broadcast | bytes 21626884 | tf_op jit(solution)/shard_map/broadcast_in_dim | solution.py:58
  177.1 0.8 bitcast_dynamic-update-slice_fusion
  177.9 1.8 fusion.24
  179.6 1.7 fusion.23
  181.4 8.6 %convert.4 = bf16[66,5,128,128]{3,2,1,0:T(8,128)(2,1)S(1)} convert(f32[66,5,128,128]{3,2,1,0:T(8,128)} %fusion.23) | non-fusion elementwise | flops 5406720 | bytes 32440320 | tf_op jit(solution)/shard_map/convert.1
  190.0 1.6 collective-permute-start
  191.5 3.2 copy-done.2
  194.8 7.4 %slice.156 = f32[64,5,128,128]{3,2,1,0:T(8,128)} slice(f32[66,5,128,128]{3,2,1,0:T(8,128)S(1)} %copy-done.2), slice={[1:65], [0:5], [0:128], [0:128]} | slice | bytes 41943040 | tf_op jit(solution)/shard_map/slice | solution.py:68
  202.2 1.3 collective-permute-start.1
  203.5 0.8 fusion.22
  204.2 1.2 collective-permute-done.1
  205.4 1.7 fusion.21
  207.2 16.1 %copy.13 = f32[64,5,128,128]{3,2,0,1:T(8,128)} copy(f32[64,5,128,128]{3,2,1,0:T(8,128)} %fusion.21) | data formatting | bytes 41943040 | tf_op jit(solution)/shard_map/scatter-add | solution.py:72
  223.3 22.7 %reshape.247 = f32[64,5,16384]{2,0,1:T(8,128)} reshape(f32[64,5,128,128]{3,2,0,1:T(8,128)} %copy.13) | data formatting | bytes 41943040 | tf_op jit(solution)/shard_map/reshape | solution.py:73
  245.9 401.1 %reduce-scatter.2.cloned.1.call-done = f32[64,5,256]{2,0,1:T(8,128)} async-done(((f32[64,5,16384]{2,0,1:T(8,128)}), f32[64,5,256]{2,0,1:T(8,128)}) %reduce-scatter.2.cloned.1.call-update) | async-done | bytes 327696 | tf_op jit(solution)/shard_map/reduce_scatter | solution.py:74
  (43 shorter events, 17.0 us)
Async XLA Ops:
  6.5 9.1 %copy-start = (bf16[64,128,128]{2,1,0:T(8,128)(2,1)S(1)}, bf16[64,128,128]{2,1,0:T(8,128)(2,1)}, u32[]{:S(2)}) copy-start(bf16[64,128,128]{2,1,0:T(8,128)(2,1)} %param.10) | copy-start | bytes 6291460
  61.7 12.1 %copy-start.4 = (s32[64]{0:T(128)S(1)}, s32[64]{0:T(128)}, u32[]{:S(2)}) copy-start(s32[64]{0:T(128)} %param.11) | copy-start | bytes 772
  61.7 92.6 %copy-start.3 = (bf16[64,64]{1,0:T(8,128)(2,1)S(1)}, bf16[64,64]{1,0:T(8,128)(2,1)}, u32[]{:S(2)}) copy-start(bf16[64,64]{1,0:T(8,128)(2,1)} %param.13) | copy-start | bytes 24580
  61.7 92.6 %all-to-all-start = ((bf16[64,1,1,3,128,128]{5,4,3,2,1,0:T(8,128)(2,1)}), bf16[64,1,1,3,128,128]{5,4,3,2,1,0:T(8,128)(2,1)}, u32[]{:S(2)}, u32[]{:S(2)}) async-start(bf16[64,1,1,3,128,128]{5,4,3,2,1,0:T(8,128)(2,1)} %constant_dynamic-update-slice_fusion), calls=%async_computation | async-start | bytes 12582912 | tf_op jit(solution)/shard_map/all_to_all | solution.py:10
  73.5 573.5 %reduce-scatter.2.cloned.1.call-start = ((), (), s32[]{:S(2)}) async-start(), calls=%async_computation.2 | async-start | bytes 21299200 | tf_op jit(solution)/shard_map/reduce_scatter | solution.py:74
  181.4 13.4 %copy-start.2 = (f32[66,5,128,128]{3,2,1,0:T(8,128)S(1)}, f32[66,5,128,128]{3,2,1,0:T(8,128)}, u32[]{:S(2)}) copy-start(f32[66,5,128,128]{3,2,1,0:T(8,128)} %fusion.23) | copy-start | bytes 64880644
  190.0 13.5 %collective-permute-start = (bf16[1,5,128,128]{3,2,1,0:T(8,128)(2,1)S(1)}, bf16[1,5,128,128]{3,2,1,0:T(8,128)(2,1)S(1)}, u32[]{:S(2)}, u32[]{:S(2)}) collective-permute-start(bf16[1,5,128,128]{3,2,1,0:T(8,128)(2,1)S(1)} %get-tuple-element.30), channel_id=1, source_target_pairs={{0,1},{2,3},{4,5},{6,7},{8,9},{10,11},{12,13},{14,15},{16,17},{18,... | collective-permute-start | bytes 491528 | tf_op jit(solution)/shard_map/ppermute | solution.py:17
  202.2 3.3 collective-permute-start.1
  245.9 401.2 %copy-start.1 = (bf16[64,128,128]{2,1,0:T(8,128)(2,1)S(1)}, bf16[64,128,128]{2,1,0:T(8,128)(2,1)}, u32[]{:S(2)}) copy-start(bf16[64,128,128]{2,1,0:T(8,128)(2,1)} %param.10) | copy-start | bytes 6291460
Sparse Core Ops, SparseCore 0:
  246.1 400.9 reduce-scatter.1
